TPU v7x, 256 devices: a whole 4x4x8 slice. The times are simulated.
256 devices in a mesh: row: 16 (over x_hi, z), col: 16 (over y, x_lo, core).
Axes of the slice: x: 4 (x_hi: 2, x_lo: 2; x = x_hi * 2 + x_lo), y: 4, z: 8, core: 2. Of those that a mesh axis runs over, the one named last changes fastest.
Arguments:
- node_feats: bfloat16 [65536, 256], P(('row', 'col')), may hold values from -6 to 6
- dest_grad: bfloat16 [16, 4096, 256], P('col', 'row'), may hold values from -6 to 6
- bases: bfloat16 [30, 256, 256], replicated, may hold values from -0.375 to 0.375
- coefs: bfloat16 [2000, 30], replicated, may hold values from -1 to 1
- src_ids: int32 [16, 16, 1024], P('row', 'col'), may hold values from 0 to 4095
- dst_ids: int32 [16, 16, 1024], P('row', 'col'), may hold values from 0 to 4095
- rel_ids: int32 [16, 16, 1024], P('row', 'col'), may hold values from 0 to 1999
- edge_norm: float32 [16, 16, 1024], P('row', 'col'), may hold values from 0.1 to 1
- block_fill: int32 [16, 16, 8], P('row', 'col'), may hold values from 0 to 128, as said below
Outputs:
- node_grad: bfloat16 [65536, 256], P(('row', 'col'))
- basis_grad: float32 [7680, 256], P(('row', 'col'))
- coef_grad: float32 [2000, 30], replicated
Inputs may be any that keep to these rules, and one draw needn't show every extreme that they name: `block_fill`: the first block of every device is full, and blocks after a device's last live block are empty.
All inputs are finite; a program needn't handle non-finite values.
Results may differ from a plain program's by a relative error of at most 0.0049.
Values may be sent and summed in bfloat16 or wider, within the bound.
A program may use at most 64 MiB of HBM per device.

v0:
```python
import jax
import jax.numpy as jnp
from jax import lax
from jax.sharding import PartitionSpec as P

EDGE_BLOCK = 128


def on_device(
    node_feats, dest_grad, bases, coefs, src_ids, dst_ids, rel_ids, edge_norm, block_fill
):
    col_count = lax.axis_size("col")
    source_rows = lax.all_gather(node_feats, "col", axis=0, tiled=True)
    target_rows = lax.all_gather(dest_grad[0], "row", axis=0, tiled=True)
    sources = src_ids.reshape(-1)
    targets = dst_ids.reshape(-1)
    relations = rel_ids.reshape(-1)
    fills = block_fill.reshape(-1)
    block_total = fills.shape[0]
    position = lax.broadcasted_iota(jnp.int32, (block_total, EDGE_BLOCK), 1)
    live_mask = (position < fills[:, None]).reshape(-1).astype(jnp.float32)
    weights = edge_norm.reshape(-1) * live_mask
    edge_total = sources.shape[0]
    edge_grad = (weights[:, None] * target_rows[targets].astype(jnp.float32)).astype(jnp.bfloat16)
    edge_rows = source_rows[sources]
    edge_coefs = coefs[relations]
    basis_count = bases.shape[0]
    width = bases.shape[1]
    vertex_count = source_rows.shape[0]
    relation_count = coefs.shape[0]
    block_span = 512
    node_part = jnp.zeros((vertex_count, width), jnp.float32)
    coef_part = jnp.zeros((relation_count, basis_count), jnp.float32)
    for offset in range(0, edge_total, block_span):
        grad_block = edge_grad[offset : offset + block_span]
        rows_block = edge_rows[offset : offset + block_span]
        coef_block = edge_coefs[offset : offset + block_span].astype(jnp.float32)
        backed = lax.dot_general(
            grad_block, bases, (((1,), (2,)), ((), ())), preferred_element_type=jnp.float32
        )
        per_edge = jnp.sum(coef_block[:, :, None] * backed, axis=1)
        inner = jnp.sum(backed * rows_block[:, None, :].astype(jnp.float32), axis=2)
        node_part = node_part + jax.ops.segment_sum(
            per_edge, sources[offset : offset + block_span], num_segments=vertex_count
        )
        coef_part = coef_part + jax.ops.segment_sum(
            inner, relations[offset : offset + block_span], num_segments=relation_count
        )
    node_grad = lax.psum_scatter(node_part, "col", scatter_dimension=0, tiled=True).astype(
        jnp.bfloat16
    )
    basis_rows = (edge_coefs[:, :, None] * edge_rows[:, None, :]).reshape(
        edge_total, basis_count * width
    )
    basis_grad = lax.psum_scatter(
        lax.dot_general(
            basis_rows, edge_grad, (((0,), (0,)), ((), ())), preferred_element_type=jnp.float32
        ),
        ("row", "col"),
        scatter_dimension=0,
        tiled=True,
    )
    coef_grad = lax.psum(coef_part, ("row", "col"))
    return (node_grad, basis_grad / col_count, coef_grad / col_count)


def solution(mesh):
    in_specs = (
        P(("row", "col"), None),
        P("col", "row", None),
        P(),
        P(),
        P("row", "col", None),
        P("row", "col", None),
        P("row", "col", None),
        P("row", "col", None),
        P("row", "col", None),
    )
    out_specs = (P(("row", "col"), None), P(("row", "col"), None), P())
    return jax.shard_map(
        on_device, mesh=mesh, in_specs=in_specs, out_specs=out_specs, check_vma=False
    )
```

profile of v0, /device:TPU:4, one launch (start us, length us, event | category | flops | bytes accessed | tf_op | source)
XLA Modules:
  0.0 924.1 jit_solution(12984734901086320531)
XLA Ops:
  10.6 3.2 gather_fusion
  17.6 31.2 %all-gather.4.cloned.1.call-done = bf16[4096,256]{1,0:T(8,128)(2,1)} async-done(((bf16[256,256]{1,0:T(8,128)(2,1)}), bf16[4096,256]{1,0:T(8,128)(2,1)}) %all-gather.4.cloned.1.call-update) | async-done | bytes 2097168 | tf_op jit(solution)/shard_map/all_gather | solution.py:13
  48.8 5.3 gather_fusion.2
  54.6 80.1 %all-gather.6.cloned.1.call-done = bf16[1,4096,256]{2,1,0:T(8,128)(2,1)} async-done(((bf16[1,256,256]{2,1,0:T(8,128)(2,1)}), bf16[1,4096,256]{2,1,0:T(8,128)(2,1)}) %all-gather.6.cloned.1.call-update) | async-done | bytes 2097168 | tf_op jit(solution)/shard_map/all_gather | solution.py:14
  134.7 5.3 gather_fusion.1
  140.2 6.3 multiply_reduce_fusion
  146.5 4.2 multiply_reduce_fusion.1
  151.0 7.0 scatter_custom_fusion.1
  159.7 8.3 scatter_custom_fusion
  168.2 4.1 broadcast_multiply_fusion
  172.3 6.7 fusion.9
  179.0 597.6 %fusion = f32[32,256]{1,0:T(8,128)S(1)} fusion(f32[7680,256]{1,0:T(8,128)} %fusion.9), kind=kCustom, calls=%all-reduce-scatter | all-reduce-scatter fusion | flops 2097153 | bytes 7897088
  786.3 6.7 collective-permute-start.10
  793.0 8.1 collective-permute-start.9
  803.1 14.8 %collective-permute-start.7 = (f32[32,256]{1,0:T(8,128)S(1)}, f32[32,256]{1,0:T(8,128)S(1)}, u32[]{:S(2)}, u32[]{:S(2)}) collective-permute-start(f32[32,256]{1,0:T(8,128)S(1)} %fusion), channel_id=1, source_target_pairs={{0,8},{1,9},{2,10},{3,11},{4,12},{5,13},{6,14},{7,15},{8,16},{9,17... | collective-permute-start | bytes 98312
  817.9 27.8 %collective-permute-start.6 = (f32[32,256]{1,0:T(8,128)S(1)}, f32[32,256]{1,0:T(8,128)S(1)}, u32[]{:S(2)}, u32[]{:S(2)}) collective-permute-start(f32[32,256]{1,0:T(8,128)S(1)} %fusion), channel_id=1, source_target_pairs={{0,7},{1,8},{2,9},{3,10},{4,11},{5,12},{6,13},{7,14},{8,15},{9,16}... | collective-permute-start | bytes 98312
  845.8 24.3 %collective-permute-start.5 = (f32[32,256]{1,0:T(8,128)S(1)}, f32[32,256]{1,0:T(8,128)S(1)}, u32[]{:S(2)}, u32[]{:S(2)}) collective-permute-start(f32[32,256]{1,0:T(8,128)S(1)} %fusion), channel_id=1, source_target_pairs={{0,6},{1,7},{2,8},{3,9},{4,10},{5,11},{6,12},{7,13},{8,14},{9,15},... | collective-permute-start | bytes 98312
  870.1 17.0 %collective-permute-start.4 = (f32[32,256]{1,0:T(8,128)S(1)}, f32[32,256]{1,0:T(8,128)S(1)}, u32[]{:S(2)}, u32[]{:S(2)}) collective-permute-start(f32[32,256]{1,0:T(8,128)S(1)} %fusion), channel_id=1, source_target_pairs={{0,5},{1,6},{2,7},{3,8},{4,9},{5,10},{6,11},{7,12},{8,13},{9,14},{... | collective-permute-start | bytes 98312
  887.1 2.5 collective-permute-start.3
  889.6 8.7 collective-permute-start.2
  898.3 3.0 collective-permute-start.1
  903.4 3.7 collective-permute-done.2
  908.4 2.5 collective-permute-done
  910.9 2.1 concatenate.16
  (61 shorter events, 29.3 us)
Async XLA Ops:
  7.2 41.6 %all-gather.4.cloned.1.call-start = ((), (), s32[]{:S(2)}) async-start(), calls=%async_computation.2 | async-start | bytes 2228224 | tf_op jit(solution)/shard_map/all_gather | solution.py:13
  7.9 126.8 %all-gather.6.cloned.1.call-start = ((), (), s32[]{:S(2)}) async-start(), calls=%async_computation.4 | async-start | bytes 2228224 | tf_op jit(solution)/shard_map/all_gather | solution.py:14
  8.6 904.9 %all-reduce.4.cloned.1.call-start = ((), (), s32[]{:S(2)}) async-start(), calls=%async_computation.3 | async-start | bytes 2048000 | tf_op jit(solution)/shard_map/psum | solution.py:63
  140.2 6.3 copy-start
  158.0 757.9 %reduce-scatter.4.cloned.1.call-start = ((), (), s32[]{:S(2)}) async-start(), calls=%async_computation.1 | async-start | bytes 4456448 | tf_op jit(solution)/shard_map/reduce_scatter | solution.py:49
  776.6 9.6 %collective-permute-start.15 = (f32[30,256]{1,0:T(8,128)S(1)}, f32[30,256]{1,0:T(8,128)S(1)}, u32[]{:S(2)}, u32[]{:S(2)}) collective-permute-start(f32[30,256]{1,0:T(8,128)S(1)} %slice.56), channel_id=1, source_target_pairs={{0,16},{1,17},{2,18},{3,19},{4,20},{5,21},{6,22},{7,23},{8,24},{9,... | collective-permute-start | bytes 92168
  778.6 14.5 %collective-permute-start.14 = (f32[32,256]{1,0:T(8,128)S(1)}, f32[32,256]{1,0:T(8,128)S(1)}, u32[]{:S(2)}, u32[]{:S(2)}) collective-permute-start(f32[32,256]{1,0:T(8,128)S(1)} %fusion), channel_id=1, source_target_pairs={{0,15},{1,16},{2,17},{3,18},{4,19},{5,20},{6,21},{7,22},{8,23},{9,... | collective-permute-start | bytes 98312
  780.5 20.6 %collective-permute-start.13 = (f32[32,256]{1,0:T(8,128)S(1)}, f32[32,256]{1,0:T(8,128)S(1)}, u32[]{:S(2)}, u32[]{:S(2)}) collective-permute-start(f32[32,256]{1,0:T(8,128)S(1)} %fusion), channel_id=1, source_target_pairs={{0,14},{1,15},{2,16},{3,17},{4,18},{5,19},{6,20},{7,21},{8,22},{9,... | collective-permute-start | bytes 98312
  782.4 20.6 %collective-permute-start.12 = (f32[32,256]{1,0:T(8,128)S(1)}, f32[32,256]{1,0:T(8,128)S(1)}, u32[]{:S(2)}, u32[]{:S(2)}) collective-permute-start(f32[32,256]{1,0:T(8,128)S(1)} %fusion), channel_id=1, source_target_pairs={{0,13},{1,14},{2,15},{3,16},{4,17},{5,18},{6,19},{7,20},{8,21},{9,... | collective-permute-start | bytes 98312
  784.3 33.6 %collective-permute-start.11 = (f32[32,256]{1,0:T(8,128)S(1)}, f32[32,256]{1,0:T(8,128)S(1)}, u32[]{:S(2)}, u32[]{:S(2)}) collective-permute-start(f32[32,256]{1,0:T(8,128)S(1)} %fusion), channel_id=1, source_target_pairs={{0,12},{1,13},{2,14},{3,15},{4,16},{5,17},{6,18},{7,19},{8,20},{9,... | collective-permute-start | bytes 98312
  786.3 59.5 %collective-permute-start.10 = (f32[32,256]{1,0:T(8,128)S(1)}, f32[32,256]{1,0:T(8,128)S(1)}, u32[]{:S(2)}, u32[]{:S(2)}) collective-permute-start(f32[32,256]{1,0:T(8,128)S(1)} %fusion), channel_id=1, source_target_pairs={{0,11},{1,12},{2,13},{3,14},{4,15},{5,16},{6,17},{7,18},{8,19},{9,... | collective-permute-start | bytes 98312
  793.0 77.1 %collective-permute-start.9 = (f32[32,256]{1,0:T(8,128)S(1)}, f32[32,256]{1,0:T(8,128)S(1)}, u32[]{:S(2)}, u32[]{:S(2)}) collective-permute-start(f32[32,256]{1,0:T(8,128)S(1)} %fusion), channel_id=1, source_target_pairs={{0,10},{1,11},{2,12},{3,13},{4,14},{5,15},{6,16},{7,17},{8,18},{9,... | collective-permute-start | bytes 98312
  801.1 86.0 %collective-permute-start.8 = (f32[32,256]{1,0:T(8,128)S(1)}, f32[32,256]{1,0:T(8,128)S(1)}, u32[]{:S(2)}, u32[]{:S(2)}) collective-permute-start(f32[32,256]{1,0:T(8,128)S(1)} %fusion), channel_id=1, source_target_pairs={{0,9},{1,10},{2,11},{3,12},{4,13},{5,14},{6,15},{7,16},{8,17},{9,1... | collective-permute-start | bytes 98312
  803.1 86.6 %collective-permute-start.7 = (f32[32,256]{1,0:T(8,128)S(1)}, f32[32,256]{1,0:T(8,128)S(1)}, u32[]{:S(2)}, u32[]{:S(2)}) collective-permute-start(f32[32,256]{1,0:T(8,128)S(1)} %fusion), channel_id=1, source_target_pairs={{0,8},{1,9},{2,10},{3,11},{4,12},{5,13},{6,14},{7,15},{8,16},{9,17... | collective-permute-start | bytes 98312
  817.9 80.4 %collective-permute-start.6 = (f32[32,256]{1,0:T(8,128)S(1)}, f32[32,256]{1,0:T(8,128)S(1)}, u32[]{:S(2)}, u32[]{:S(2)}) collective-permute-start(f32[32,256]{1,0:T(8,128)S(1)} %fusion), channel_id=1, source_target_pairs={{0,7},{1,8},{2,9},{3,10},{4,11},{5,12},{6,13},{7,14},{8,15},{9,16}... | collective-permute-start | bytes 98312
  845.8 55.6 %collective-permute-start.5 = (f32[32,256]{1,0:T(8,128)S(1)}, f32[32,256]{1,0:T(8,128)S(1)}, u32[]{:S(2)}, u32[]{:S(2)}) collective-permute-start(f32[32,256]{1,0:T(8,128)S(1)} %fusion), channel_id=1, source_target_pairs={{0,6},{1,7},{2,8},{3,9},{4,10},{5,11},{6,12},{7,13},{8,14},{9,15},... | collective-permute-start | bytes 98312
  870.1 33.2 %collective-permute-start.4 = (f32[32,256]{1,0:T(8,128)S(1)}, f32[32,256]{1,0:T(8,128)S(1)}, u32[]{:S(2)}, u32[]{:S(2)}) collective-permute-start(f32[32,256]{1,0:T(8,128)S(1)} %fusion), channel_id=1, source_target_pairs={{0,5},{1,6},{2,7},{3,8},{4,9},{5,10},{6,11},{7,12},{8,13},{9,14},{... | collective-permute-start | bytes 98312
  887.1 16.3 %collective-permute-start.3 = (f32[32,256]{1,0:T(8,128)S(1)}, f32[32,256]{1,0:T(8,128)S(1)}, u32[]{:S(2)}, u32[]{:S(2)}) collective-permute-start(f32[32,256]{1,0:T(8,128)S(1)} %fusion), channel_id=1, source_target_pairs={{0,4},{1,5},{2,6},{3,7},{4,8},{5,9},{6,10},{7,11},{8,12},{9,13},{1... | collective-permute-start | bytes 98312
  889.6 17.5 %collective-permute-start.2 = (f32[32,256]{1,0:T(8,128)S(1)}, f32[32,256]{1,0:T(8,128)S(1)}, u32[]{:S(2)}, u32[]{:S(2)}) collective-permute-start(f32[32,256]{1,0:T(8,128)S(1)} %fusion), channel_id=1, source_target_pairs={{0,3},{1,4},{2,5},{3,6},{4,7},{5,8},{6,9},{7,10},{8,11},{9,12},{10... | collective-permute-start | bytes 98312
  898.3 10.0 %collective-permute-start.1 = (f32[32,256]{1,0:T(8,128)S(1)}, f32[32,256]{1,0:T(8,128)S(1)}, u32[]{:S(2)}, u32[]{:S(2)}) collective-permute-start(f32[32,256]{1,0:T(8,128)S(1)} %fusion), channel_id=1, source_target_pairs={{0,2},{1,3},{2,4},{3,5},{4,6},{5,7},{6,8},{7,9},{8,10},{9,11},{10,... | collective-permute-start | bytes 98312
  901.4 9.5 %collective-permute-start = (f32[32,256]{1,0:T(8,128)S(1)}, f32[32,256]{1,0:T(8,128)S(1)}, u32[]{:S(2)}, u32[]{:S(2)}) collective-permute-start(f32[32,256]{1,0:T(8,128)S(1)} %fusion), channel_id=1, source_target_pairs={{0,1},{1,2},{2,3},{3,4},{4,5},{5,6},{6,7},{7,8},{8,9},{9,10},{10,1... | collective-permute-start | bytes 98312
Sparse Core Ops, SparseCore 0:
  9.8 38.8 all-gather.3
  51.3 83.2 all-gather.5
  158.1 258.4 all-reduce.3
  419.0 74.0 reduce-scatter.3
where the time goes:
time: 925 us; the launch traced here: 924 us
  blocking collectives  598 us (65%)
  starting transfers between devices  127 us (14%)
  waiting for transfers between devices  120 us (13%)
  other arithmetic  27.4 us (3%)
  local copies, waits for them, and re-layouts  20.9 us (2%)
  matrix products  17.1 us (2%)
  between operations  14.1 us (2%)
    unnamed x1, blocking collectives  598 us
    unnamed x16, starting transfers between devices  126 us
    all_gather x1, waiting for transfers between devices, on_device(): target_rows = lax.all_gather(dest_grad[0], 'row', axis=0, tiled=True)  80.1 us
    all_gather x1, waiting for transfers between devices, on_device(): source_rows = lax.all_gather(node_feats, 'col', axis=0, tiled=True)  31.2 us
  transfers between devices with their start and end apart: 20, of which 5 were waited for; matrix products, arithmetic and copies ran while one was open for 69% of the time, Pallas kernels for 0%

commit v1 on v0

--- a/solution.py
+++ b/solution.py
@@ -11,7 +11,9 @@
 ):
     col_count = lax.axis_size("col")
     source_rows = lax.all_gather(node_feats, "col", axis=0, tiled=True)
-    target_rows = lax.all_gather(dest_grad[0], "row", axis=0, tiled=True)
+    target_rows = jnp.concatenate(
+        lax.all_to_all(jnp.stack([dest_grad[0]] * lax.axis_size("row")), "row", 0, 0), axis=0
+    )
     sources = src_ids.reshape(-1)
     targets = dst_ids.reshape(-1)
     relations = rel_ids.reshape(-1)

time: 925 us -> 856 us (0.925)
  waiting for transfers between devices: 120 us -> 42.2 us
  starting transfers between devices: 127 us -> 138 us
    all_gather x1 -> x0, waiting for transfers between devices: 80.1 us -> none  [on_device(): target_rows = lax.all_gather(dest_grad[0], 'row', axis=0, tiled=True)]
    all_to_all x0 -> x1, starting transfers between devices: none -> 11.4 us  [on_device(): lax.all_to_all(jnp.stack([dest_grad[0]] * lax.axis_size('row')), 'row', 0...]
  transfers between devices with their start and end apart: 20 -> 20, of which waited for: 5 -> 5; matrix products, arithmetic and copies ran while one was open for 69% -> 75% of each run, Pallas kernels for 0% -> 0%
where the time goes in v1:
time: 856 us; the launch traced here: 855 us
  blocking collectives  597 us (70%)
  starting transfers between devices  138 us (16%)
  waiting for transfers between devices  42.2 us (5%)
  other arithmetic  24.9 us (3%)
  local copies, waits for them, and re-layouts  23.3 us (3%)
  matrix products  15.6 us (2%)
  between operations  14.3 us (2%)
    unnamed x1, blocking collectives  597 us
    unnamed x16, starting transfers between devices  126 us
    all_gather x1, waiting for transfers between devices, on_device(): source_rows = lax.all_gather(node_feats, 'col', axis=0, tiled=True)  28.5 us
  transfers between devices with their start and end apart: 20, of which 5 were waited for; matrix products, arithmetic and copies ran while one was open for 75% of the time, Pallas kernels for 0%

profile of v1, /device:TPU:4, one launch (start us, length us, event | category | flops | bytes accessed | tf_op | source)
XLA Modules:
  0.0 855.2 jit_solution(10719383880357969187)
XLA Ops:
  10.4 11.4 %all-to-all-start = ((bf16[16,256,256]{2,1,0:T(8,128)(2,1)}), bf16[16,256,256]{2,1,0:T(8,128)(2,1)S(1)}, u32[]{:S(2)}, u32[]{:S(2)}) async-start(bf16[16,256,256]{2,1,0:T(8,128)(2,1)} %stack.3), calls=%async_computation | async-start | bytes 4194304 | tf_op jit(solution)/shard_map/all_to_all | solution.py:15
  23.8 3.2 gather_fusion
  27.4 28.5 %all-gather.2.cloned.1.call-done = bf16[4096,256]{1,0:T(8,128)(2,1)} async-done(((bf16[256,256]{1,0:T(8,128)(2,1)}), bf16[4096,256]{1,0:T(8,128)(2,1)}) %all-gather.2.cloned.1.call-update) | async-done | bytes 2097168 | tf_op jit(solution)/shard_map/all_gather | solution.py:13
  55.9 5.3 gather_fusion.2
  65.1 5.5 all-to-all-done
  70.7 3.9 gather_fusion.1
  74.9 5.5 multiply_reduce_fusion
  80.4 3.4 multiply_reduce_fusion.1
  84.1 7.0 scatter_custom_fusion.1
  91.6 8.3 scatter_custom_fusion
  100.1 4.1 broadcast_multiply_fusion
  104.2 6.6 fusion.9
  110.9 597.2 %fusion = f32[32,256]{1,0:T(8,128)S(1)} fusion(f32[7680,256]{1,0:T(8,128)} %fusion.9), kind=kCustom, calls=%all-reduce-scatter | all-reduce-scatter fusion | flops 2097153 | bytes 7897088
  717.8 8.0 collective-permute-start.10
  725.8 7.8 collective-permute-start.9
  735.5 13.5 %collective-permute-start.7 = (f32[32,256]{1,0:T(8,128)S(1)}, f32[32,256]{1,0:T(8,128)S(1)}, u32[]{:S(2)}, u32[]{:S(2)}) collective-permute-start(f32[32,256]{1,0:T(8,128)S(1)} %fusion), channel_id=1, source_target_pairs={{0,8},{1,9},{2,10},{3,11},{4,12},{5,13},{6,14},{7,15},{8,16},{9,17... | collective-permute-start | bytes 98312
  749.0 27.9 %collective-permute-start.6 = (f32[32,256]{1,0:T(8,128)S(1)}, f32[32,256]{1,0:T(8,128)S(1)}, u32[]{:S(2)}, u32[]{:S(2)}) collective-permute-start(f32[32,256]{1,0:T(8,128)S(1)} %fusion), channel_id=1, source_target_pairs={{0,7},{1,8},{2,9},{3,10},{4,11},{5,12},{6,13},{7,14},{8,15},{9,16}... | collective-permute-start | bytes 98312
  776.9 24.3 %collective-permute-start.5 = (f32[32,256]{1,0:T(8,128)S(1)}, f32[32,256]{1,0:T(8,128)S(1)}, u32[]{:S(2)}, u32[]{:S(2)}) collective-permute-start(f32[32,256]{1,0:T(8,128)S(1)} %fusion), channel_id=1, source_target_pairs={{0,6},{1,7},{2,8},{3,9},{4,10},{5,11},{6,12},{7,13},{8,14},{9,15},... | collective-permute-start | bytes 98312
  801.3 16.5 %collective-permute-start.4 = (f32[32,256]{1,0:T(8,128)S(1)}, f32[32,256]{1,0:T(8,128)S(1)}, u32[]{:S(2)}, u32[]{:S(2)}) collective-permute-start(f32[32,256]{1,0:T(8,128)S(1)} %fusion), channel_id=1, source_target_pairs={{0,5},{1,6},{2,7},{3,8},{4,9},{5,10},{6,11},{7,12},{8,13},{9,14},{... | collective-permute-start | bytes 98312
  817.8 3.0 collective-permute-start.3
  820.8 8.7 %collective-permute-start.2 = (f32[32,256]{1,0:T(8,128)S(1)}, f32[32,256]{1,0:T(8,128)S(1)}, u32[]{:S(2)}, u32[]{:S(2)}) collective-permute-start(f32[32,256]{1,0:T(8,128)S(1)} %fusion), channel_id=1, source_target_pairs={{0,3},{1,4},{2,5},{3,6},{4,7},{5,8},{6,9},{7,10},{8,11},{9,12},{10... | collective-permute-start | bytes 98312
  829.5 3.0 collective-permute-start.1
  834.5 3.7 collective-permute-done.2
  839.6 2.5 collective-permute-done
  (77 shorter events, 31.9 us)
Async XLA Ops:
  7.2 20.0 %copy-start.3 = (s32[1,1,1024]{2,1,0:T(1,128)S(1)}, s32[1,1,1024]{2,1,0:T(1,128)}, u32[]{:S(2)}) copy-start(s32[1,1,1024]{2,1,0:T(1,128)} %param.15) | copy-start | bytes 12292
  7.2 20.1 %copy-start.5 = (s32[1,1,1024]{2,1,0:T(1,128)S(1)}, s32[1,1,1024]{2,1,0:T(1,128)}, u32[]{:S(2)}) copy-start(s32[1,1,1024]{2,1,0:T(1,128)} %param.14) | copy-start | bytes 12292
  7.2 20.1 %copy-start.6 = (f32[1,1,1024]{2,1,0:T(1,128)S(1)}, f32[1,1,1024]{2,1,0:T(1,128)}, u32[]{:S(2)}) copy-start(f32[1,1,1024]{2,1,0:T(1,128)} %param.16) | copy-start | bytes 12292
  7.2 20.1 %copy-start.7 = (s32[1,1,8]{2,1,0:T(1,128)S(1)}, s32[1,1,8]{2,1,0:T(1,128)}, u32[]{:S(2)}) copy-start(s32[1,1,8]{2,1,0:T(1,128)} %param.17) | copy-start | bytes 100
  7.2 48.6 %all-gather.2.cloned.1.call-start = ((), (), s32[]{:S(2)}) async-start(), calls=%async_computation.3 | async-start | bytes 2228224 | tf_op jit(solution)/shard_map/all_gather | solution.py:13
  10.4 60.3 %all-to-all-start = ((bf16[16,256,256]{2,1,0:T(8,128)(2,1)}), bf16[16,256,256]{2,1,0:T(8,128)(2,1)S(1)}, u32[]{:S(2)}, u32[]{:S(2)}) async-start(bf16[16,256,256]{2,1,0:T(8,128)(2,1)} %stack.3), calls=%async_computation | async-start | bytes 4194304 | tf_op jit(solution)/shard_map/all_to_all | solution.py:15
  21.8 822.9 %all-reduce.4.cloned.1.call-start = ((), (), s32[]{:S(2)}) async-start(), calls=%async_computation.4 | async-start | bytes 2048000 | tf_op jit(solution)/shard_map/psum | solution.py:65
  91.1 756.0 %reduce-scatter.4.cloned.1.call-start = ((), (), s32[]{:S(2)}) async-start(), calls=%async_computation.2 | async-start | bytes 4456448 | tf_op jit(solution)/shard_map/reduce_scatter | solution.py:51
  708.1 9.6 %collective-permute-start.15 = (f32[30,256]{1,0:T(8,128)S(1)}, f32[30,256]{1,0:T(8,128)S(1)}, u32[]{:S(2)}, u32[]{:S(2)}) collective-permute-start(f32[30,256]{1,0:T(8,128)S(1)} %slice.56), channel_id=1, source_target_pairs={{0,16},{1,17},{2,18},{3,19},{4,20},{5,21},{6,22},{7,23},{8,24},{9,... | collective-permute-start | bytes 92168
  710.0 15.7 %collective-permute-start.14 = (f32[32,256]{1,0:T(8,128)S(1)}, f32[32,256]{1,0:T(8,128)S(1)}, u32[]{:S(2)}, u32[]{:S(2)}) collective-permute-start(f32[32,256]{1,0:T(8,128)S(1)} %fusion), channel_id=1, source_target_pairs={{0,15},{1,16},{2,17},{3,18},{4,19},{5,20},{6,21},{7,22},{8,23},{9,... | collective-permute-start | bytes 98312
  712.0 21.6 %collective-permute-start.13 = (f32[32,256]{1,0:T(8,128)S(1)}, f32[32,256]{1,0:T(8,128)S(1)}, u32[]{:S(2)}, u32[]{:S(2)}) collective-permute-start(f32[32,256]{1,0:T(8,128)S(1)} %fusion), channel_id=1, source_target_pairs={{0,14},{1,15},{2,16},{3,17},{4,18},{5,19},{6,20},{7,21},{8,22},{9,... | collective-permute-start | bytes 98312
  713.9 21.6 %collective-permute-start.12 = (f32[32,256]{1,0:T(8,128)S(1)}, f32[32,256]{1,0:T(8,128)S(1)}, u32[]{:S(2)}, u32[]{:S(2)}) collective-permute-start(f32[32,256]{1,0:T(8,128)S(1)} %fusion), channel_id=1, source_target_pairs={{0,13},{1,14},{2,15},{3,16},{4,17},{5,18},{6,19},{7,20},{8,21},{9,... | collective-permute-start | bytes 98312
  715.8 33.2 %collective-permute-start.11 = (f32[32,256]{1,0:T(8,128)S(1)}, f32[32,256]{1,0:T(8,128)S(1)}, u32[]{:S(2)}, u32[]{:S(2)}) collective-permute-start(f32[32,256]{1,0:T(8,128)S(1)} %fusion), channel_id=1, source_target_pairs={{0,12},{1,13},{2,14},{3,15},{4,16},{5,17},{6,18},{7,19},{8,20},{9,... | collective-permute-start | bytes 98312
  717.8 59.2 %collective-permute-start.10 = (f32[32,256]{1,0:T(8,128)S(1)}, f32[32,256]{1,0:T(8,128)S(1)}, u32[]{:S(2)}, u32[]{:S(2)}) collective-permute-start(f32[32,256]{1,0:T(8,128)S(1)} %fusion), channel_id=1, source_target_pairs={{0,11},{1,12},{2,13},{3,14},{4,15},{5,16},{6,17},{7,18},{8,19},{9,... | collective-permute-start | bytes 98312
  725.8 75.5 %collective-permute-start.9 = (f32[32,256]{1,0:T(8,128)S(1)}, f32[32,256]{1,0:T(8,128)S(1)}, u32[]{:S(2)}, u32[]{:S(2)}) collective-permute-start(f32[32,256]{1,0:T(8,128)S(1)} %fusion), channel_id=1, source_target_pairs={{0,10},{1,11},{2,12},{3,13},{4,14},{5,15},{6,16},{7,17},{8,18},{9,... | collective-permute-start | bytes 98312
  733.6 84.2 %collective-permute-start.8 = (f32[32,256]{1,0:T(8,128)S(1)}, f32[32,256]{1,0:T(8,128)S(1)}, u32[]{:S(2)}, u32[]{:S(2)}) collective-permute-start(f32[32,256]{1,0:T(8,128)S(1)} %fusion), channel_id=1, source_target_pairs={{0,9},{1,10},{2,11},{3,12},{4,13},{5,14},{6,15},{7,16},{8,17},{9,1... | collective-permute-start | bytes 98312
  735.5 85.3 %collective-permute-start.7 = (f32[32,256]{1,0:T(8,128)S(1)}, f32[32,256]{1,0:T(8,128)S(1)}, u32[]{:S(2)}, u32[]{:S(2)}) collective-permute-start(f32[32,256]{1,0:T(8,128)S(1)} %fusion), channel_id=1, source_target_pairs={{0,8},{1,9},{2,10},{3,11},{4,12},{5,13},{6,14},{7,15},{8,16},{9,17... | collective-permute-start | bytes 98312
  749.0 80.5 %collective-permute-start.6 = (f32[32,256]{1,0:T(8,128)S(1)}, f32[32,256]{1,0:T(8,128)S(1)}, u32[]{:S(2)}, u32[]{:S(2)}) collective-permute-start(f32[32,256]{1,0:T(8,128)S(1)} %fusion), channel_id=1, source_target_pairs={{0,7},{1,8},{2,9},{3,10},{4,11},{5,12},{6,13},{7,14},{8,15},{9,16}... | collective-permute-start | bytes 98312
  776.9 55.6 %collective-permute-start.5 = (f32[32,256]{1,0:T(8,128)S(1)}, f32[32,256]{1,0:T(8,128)S(1)}, u32[]{:S(2)}, u32[]{:S(2)}) collective-permute-start(f32[32,256]{1,0:T(8,128)S(1)} %fusion), channel_id=1, source_target_pairs={{0,6},{1,7},{2,8},{3,9},{4,10},{5,11},{6,12},{7,13},{8,14},{9,15},... | collective-permute-start | bytes 98312
  801.3 33.2 %collective-permute-start.4 = (f32[32,256]{1,0:T(8,128)S(1)}, f32[32,256]{1,0:T(8,128)S(1)}, u32[]{:S(2)}, u32[]{:S(2)}) collective-permute-start(f32[32,256]{1,0:T(8,128)S(1)} %fusion), channel_id=1, source_target_pairs={{0,5},{1,6},{2,7},{3,8},{4,9},{5,10},{6,11},{7,12},{8,13},{9,14},{... | collective-permute-start | bytes 98312
  817.8 16.7 %collective-permute-start.3 = (f32[32,256]{1,0:T(8,128)S(1)}, f32[32,256]{1,0:T(8,128)S(1)}, u32[]{:S(2)}, u32[]{:S(2)}) collective-permute-start(f32[32,256]{1,0:T(8,128)S(1)} %fusion), channel_id=1, source_target_pairs={{0,4},{1,5},{2,6},{3,7},{4,8},{5,9},{6,10},{7,11},{8,12},{9,13},{1... | collective-permute-start | bytes 98312
  820.8 17.5 %collective-permute-start.2 = (f32[32,256]{1,0:T(8,128)S(1)}, f32[32,256]{1,0:T(8,128)S(1)}, u32[]{:S(2)}, u32[]{:S(2)}) collective-permute-start(f32[32,256]{1,0:T(8,128)S(1)} %fusion), channel_id=1, source_target_pairs={{0,3},{1,4},{2,5},{3,6},{4,7},{5,8},{6,9},{7,10},{8,11},{9,12},{10... | collective-permute-start | bytes 98312
  829.5 10.0 %collective-permute-start.1 = (f32[32,256]{1,0:T(8,128)S(1)}, f32[32,256]{1,0:T(8,128)S(1)}, u32[]{:S(2)}, u32[]{:S(2)}) collective-permute-start(f32[32,256]{1,0:T(8,128)S(1)} %fusion), channel_id=1, source_target_pairs={{0,2},{1,3},{2,4},{3,5},{4,6},{5,7},{6,8},{7,9},{8,10},{9,11},{10,... | collective-permute-start | bytes 98312
  832.6 9.5 %collective-permute-start = (f32[32,256]{1,0:T(8,128)S(1)}, f32[32,256]{1,0:T(8,128)S(1)}, u32[]{:S(2)}, u32[]{:S(2)}) collective-permute-start(f32[32,256]{1,0:T(8,128)S(1)} %fusion), channel_id=1, source_target_pairs={{0,1},{1,2},{2,3},{3,4},{4,5},{5,6},{6,7},{7,8},{8,9},{9,10},{10,1... | collective-permute-start | bytes 98312
  (5 other events, 40.7 us)
Sparse Core Ops, SparseCore 0:
  9.9 45.9 all-gather.1
  91.2 260.6 all-reduce.3
  354.5 73.7 reduce-scatter.3
